TPU v7x, 32 devices: a whole 2x2x4 slice. The times are simulated.
32 devices in a mesh: batch: 8 (over z, core), vocab: 4 (over y, x).
Axes of the slice: x: 2, y: 2, z: 4, core: 2. Of those that a mesh axis runs over, the one named last changes fastest.
Arguments:
- hidden: bfloat16 [1024, 4096], P('batch'), may hold values from -40 to 40
- exit_layer: int32 [1024], P('batch'), may hold values from 0 to 7
- exit_gains: float32 [8, 4096], replicated, may hold values from 0.1 to 1.9
- unembed: bfloat16 [4096, 128256], P(None, ('batch', 'vocab')), may hold values from -10 to 10
- targets: int32 [1024], replicated, may hold values from 0 to 128255
- values: float32 [1024], P('batch'), may hold values from -6 to 6
- rewards: float32 [1024], P('batch'), may hold values from -2 to 2
- ref_logprob: float32 [1024], P('batch'), may hold values from -16 to -6
- segment_end: int32 [1024], P('batch'), may hold values 0 or 1
Outputs:
- logprob: float32 [1024], P('batch')
- advantages: float32 [1024], P('batch')
All inputs are finite; a program needn't handle non-finite values. No bound on the sum of `segment_end` on one device may be relied on, other than what follows from the above.
Results may differ from a plain program's by a relative error of at most 0.00054.
Values may be sent and summed in bfloat16 or wider, within the bound.
No kernel may reach another device: no remote copies, remote signals or barrier semaphores. Data moves between devices by JAX's collectives and lax.ppermute only.
A program may use at most 128 MiB of HBM per device.

v0:
```python
import jax
import jax.numpy as jnp
from jax import lax
from jax.sharding import PartitionSpec as P

epsilon_norm = 1e-05
discount = 1.0
trace_decay = 0.999
penalty_weight = 0.1


def joined(part, axis, combine):
    gathered = jax.tree.map(lambda a: lax.all_gather(a, axis), part)

    def take(source):
        return jax.tree.map(lambda a: lax.dynamic_index_in_dim(a, source, 0, False), gathered)

    return lax.fori_loop(
        1, lax.axis_size(axis), lambda source, state: combine(state, take(source)), take(0)
    )


def from_behind(value, axis, steps):
    count = lax.axis_size(axis)
    initial, last = (max(0, -steps), min(count, count - steps))
    return lax.ppermute(value, axis, [(source, source + steps) for source in range(initial, last)])


def normalize(rows, layers, exit_gains):
    states = rows.astype(jnp.float32)
    inverse = lax.rsqrt(jnp.mean(states * states, axis=-1, keepdims=True) + epsilon_norm)
    selector = (
        layers[:, None] == jnp.arange(exit_gains.shape[0], dtype=jnp.int32)[None, :]
    ).astype(jnp.float32)
    scaling = jnp.dot(selector, exit_gains, precision=lax.Precision.HIGHEST)
    return (states * inverse * scaling).astype(jnp.bfloat16)


def per_device(
    hidden, exit_layer, exit_gains, unembed, targets, values, rewards, ref_logprob, segment_end
):
    column_count = unembed.shape[1]
    column_start = lax.axis_index(("batch", "vocab")) * column_count
    columns = jnp.arange(column_count, dtype=jnp.int32)
    total_rows = targets.shape[0]
    owned = hidden.shape[0]
    peers = lax.axis_size("batch")
    width = hidden.shape[1]
    normed = normalize(hidden, exit_layer, exit_gains)
    gathered = lax.all_gather(normed, "batch", axis=0, tiled=True)
    block_rows = 512
    block_count = total_rows // block_rows

    def score_block(pair):
        rows_block, ids_block = pair
        logits = jnp.dot(rows_block, unembed, preferred_element_type=jnp.float32)
        row_max = jnp.max(logits, axis=1)
        row_total = jnp.sum(jnp.exp(logits - row_max[:, None]), axis=1)
        wanted = ids_block - column_start
        picked = jnp.sum(jnp.where(columns[None, :] == wanted[:, None], logits, 0.0), axis=1)
        return (row_max, row_total, picked)

    maxima, totals, picks = lax.map(
        score_block,
        (
            gathered.reshape(block_count, block_rows, width),
            targets.reshape(block_count, block_rows),
        ),
    )
    maxima = maxima.reshape(total_rows)
    totals = totals.reshape(total_rows)
    picks = picks.reshape(total_rows)
    maxima, totals, picks = (
        lax.all_to_all(maxima, "batch", split_axis=0, concat_axis=0, tiled=True),
        lax.all_to_all(totals, "batch", split_axis=0, concat_axis=0, tiled=True),
        lax.all_to_all(picks, "batch", split_axis=0, concat_axis=0, tiled=True),
    )
    maxima = maxima.reshape(peers, owned)
    totals = totals.reshape(peers, owned)
    picks = picks.reshape(peers, owned)
    group_max = jnp.max(maxima, axis=0)
    group_total = jnp.sum(totals * jnp.exp(maxima - group_max[None, :]), axis=0)
    group_pick = jnp.sum(picks, axis=0)

    def combine_groups(first, second):
        larger = jnp.maximum(first[0], second[0])
        summed = first[1] * jnp.exp(first[0] - larger) + second[1] * jnp.exp(second[0] - larger)
        return (larger, summed, first[2] + second[2])

    overall_max, overall_total, overall_pick = joined(
        (group_max, group_total, group_pick), "vocab", combine_groups
    )
    logprob = overall_pick - (overall_max + jnp.log(overall_total))
    following = from_behind(values[:1], "batch", -1)
    next_values = jnp.concatenate([values[1:], following])
    keeping = 1.0 - segment_end.astype(jnp.float32)
    shaped = rewards - penalty_weight * (logprob - ref_logprob)
    deltas = shaped + discount * next_values * keeping - values
    factors = discount * trace_decay * keeping

    def backward(running, inputs):
        factor, delta = inputs
        accrued = delta + factor * running[0]
        product = factor * running[1]
        return ((accrued, product), (accrued, product))

    finished, outputs = lax.scan(
        backward,
        (jnp.zeros((), jnp.float32), jnp.ones((), jnp.float32)),
        (factors, deltas),
        reverse=True,
    )
    local_adv, products = outputs
    head_adv = local_adv[:1]
    head_prod = products[:1]

    def relay_step(index, inbound):
        return from_behind(head_adv + head_prod * inbound, "batch", -1)

    incoming = lax.fori_loop(0, peers - 1, relay_step, jnp.zeros((1,), jnp.float32))
    advantages = local_adv + products * incoming
    return (logprob, advantages)


def solution(mesh):
    placed = (
        P("batch", None),
        P("batch"),
        P(),
        P(None, ("batch", "vocab")),
        P(),
        P("batch"),
        P("batch"),
        P("batch"),
        P("batch"),
    )
    return jax.shard_map(
        per_device, mesh=mesh, in_specs=placed, out_specs=(P("batch"), P("batch")), check_vma=False
    )
```

profile of v0, /device:TPU:1, one launch (start us, length us, event | category | flops | bytes accessed | tf_op | source)
XLA Modules:
  0.0 659.9 jit_solution(1969965212118673331)
XLA Ops:
  7.2 1.5 fusion.14
  8.8 3.4 fusion.13
  12.2 0.7 reshape.52
  12.9 83.9 %all-gather.8.cloned.1.call-done = bf16[1024,4096]{1,0:T(8,128)(2,1)} async-done(((bf16[128,4096]{1,0:T(8,128)(2,1)}), bf16[1024,4096]{1,0:T(8,128)(2,1)}) %all-gather.8.cloned.1.call-update) | async-done | bytes 8388624 | tf_op jit(solution)/shard_map/all_gather | solution.py:50
  96.8 49.9 %while.67 = (s32[]{:T(128)}, f32[2,512]{1,0:T(2,128)S(1)}, f32[2,512]{1,0:T(2,128)S(1)}, f32[2,512]{1,0:T(2,128)S(1)}, bf16[2,512,4096]{2,1,0:T(8,128)(2,1)}, /*...) while((s32[]{:T(128)}, f32[2,512]{1,0:T(2,128)S(1)}, ...), condition=%wide.region_5.6_spmd.clone, body=%wide.region_1.5_spmd.clone.sunk | while | flops 16823081984 | bytes 53471864 | solution.py:63
  96.9 22.6 %fusion.28 = (f32[512]{0:T(512)S(1)}, f32[512,4008]{0,1:T(8,128)S(1)}) fusion(bf16[4096,4008]{0,1:T(8,128)(2,1)} %get-tuple-element.681, bf16[2,512,4096]{2,1,0:T(8,128)(2,1)} %get-tuple-element.680, s32[]{:T(128)} %get-tuple-element.666), kind=kOutput, calls=%fused_computation.38.clone.1 | convolution fusion | flops 16812822528 | bytes 45238784 | tf_op jit(solution)/shard_map/while/body/eval_jaxpr/dot_general | solution.py:56
  119.5 2.2 select_reduce_fusion.2
  121.8 22.6 %fusion.28 = (f32[512]{0:T(512)S(1)}, f32[512,4008]{0,1:T(8,128)S(1)}) fusion(bf16[4096,4008]{0,1:T(8,128)(2,1)} %get-tuple-element.681, bf16[2,512,4096]{2,1,0:T(8,128)(2,1)} %get-tuple-element.680, s32[]{:T(128)} %get-tuple-element.666), kind=kOutput, calls=%fused_computation.38.clone.1 | convolution fusion | flops 16812822528 | bytes 45238784 | tf_op jit(solution)/shard_map/while/body/eval_jaxpr/dot_general | solution.py:56
  144.4 2.2 select_reduce_fusion.2
  147.3 3.4 all-to-all-start
  151.4 4.3 all-to-all-done
  155.7 3.9 all-to-all-start.1
  159.6 2.0 collective-permute-start.1
  162.3 2.2 all-to-all-done.1
  164.5 3.9 all-to-all-start.2
  168.4 5.9 all-gather.4
  174.3 5.9 all-gather.5
  180.2 5.0 all-gather.3
  185.3 1.1 fusion.17
  186.4 421.8 %while.65 = (s32[]{:T(128)}, f32[]{:T(128)}, f32[]{:T(128)}, f32[128]{0:T(128)S(1)}, f32[128]{0:T(128)S(1)}, /*index=5*/f32[128]{0:T(128)S(1)}, f32[128]{0:T(128)S(1)}, s32[]{:T(128)}, s32[]{:T(128)}) while((s32[]{:T(128)}, f32[]{:T(128)}, f32[]{:T(128)}, f32[128]{0:T(128)S(1)}, f32[128]{0:T(128)S(1)}, /*index=5*/f32[128]{0:T(128)S(1)}, ...), condition=%wide.region_12.13_spmd, body=%wide.region_11.12_spmd.sunk | while | flops 6 | bytes 189 | solution.py:107
  189.7 0.6 dynamic_slice.106
  196.3 0.6 dynamic_slice.106
  199.6 0.6 dynamic_slice.106
  202.9 0.6 dynamic_slice.106
  206.2 0.6 dynamic_slice.106
  209.5 0.6 dynamic_slice.106
  212.8 0.6 dynamic_slice.106
  216.1 0.6 dynamic_slice.106
  219.4 0.6 dynamic_slice.106
  222.7 0.6 dynamic_slice.106
  226.0 0.6 dynamic_slice.106
  229.3 0.6 dynamic_slice.106
  232.6 0.6 dynamic_slice.106
  608.2 44.3 %while.66 = (s32[]{:T(128)}, f32[1]{0:T(128)}, f32[1]{0:T(128)S(1)}, f32[1]{0:T(128)S(1)}, s32[]{:T(128)}) while((s32[]{:T(128)}, f32[1]{0:T(128)}, f32[1]{0:T(128)S(1)}, f32[1]{0:T(128)S(1)}, s32[]{:T(128)}) %tuple.128), condition=%wide.region_14.15_spmd, body=%wide.region_13.14_spmd.sunk | while | flops 4 | bytes 141 | solution.py:120
  608.3 9.0 %collective-permute-start = (f32[1]{0:T(128)}, f32[1]{0:T(128)}, u32[]{:S(2)}, u32[]{:S(2)}) collective-permute-start(f32[1]{0:T(128)} %add.147), channel_id=1, source_target_pairs={{4,0},{8,4},{12,8},{16,12},{20,16},{24,20},{28,24},{5,1},{9,5},{13... | collective-permute-start | bytes 20 | tf_op jit(solution)/shard_map/while/body/eval_jaxpr/ppermute | solution.py:26
  617.3 1.8 collective-permute-done
  619.8 2.9 collective-permute-start
  622.6 2.0 collective-permute-done
  625.2 2.9 collective-permute-start
  628.1 2.0 collective-permute-done
  630.7 2.9 collective-permute-start
  633.6 2.0 collective-permute-done
  636.2 2.9 collective-permute-start
  639.1 2.0 collective-permute-done
  641.7 2.9 collective-permute-start
  644.5 2.0 collective-permute-done
  647.2 2.9 collective-permute-start
  650.0 2.0 collective-permute-done
  (542 shorter events, 179.5 us)
Async XLA Ops:
  7.2 1.6 copy-start
  7.2 89.7 %all-gather.8.cloned.1.call-start = ((), (), s32[]{:S(2)}) async-start(), calls=%async_computation.3 | async-start | bytes 9437184 | tf_op jit(solution)/shard_map/all_gather | solution.py:50
  96.8 62.7 %copy-start.1 = (f32[128]{0:T(128)S(1)}, f32[128]{0:T(128)}, u32[]{:S(2)}) copy-start(f32[128]{0:T(128)} %param.22) | copy-start | bytes 1540
  96.8 88.4 %copy-start.2 = (f32[128]{0:T(128)S(1)}, f32[128]{0:T(128)}, u32[]{:S(2)}) copy-start(f32[128]{0:T(128)} %param.23) | copy-start | bytes 1540
  96.8 88.4 %copy-start.3 = (f32[128]{0:T(128)S(1)}, f32[128]{0:T(128)}, u32[]{:S(2)}) copy-start(f32[128]{0:T(128)} %param.24) | copy-start | bytes 1540
  96.8 88.4 %copy-start.4 = (s32[128]{0:T(128)S(1)}, s32[128]{0:T(128)}, u32[]{:S(2)}) copy-start(s32[128]{0:T(128)} %param.25) | copy-start | bytes 1540
  147.3 8.4 %all-to-all-start = ((f32[8,128,1]{1,2,0:T(1,128)}), f32[8,128,1]{1,2,0:T(1,128)S(1)}, u32[]{:S(2)}, u32[]{:S(2)}) async-start(f32[8,128,1]{1,2,0:T(1,128)} %all_to_all.18), calls=%async_computation | async-start | bytes 8192 | tf_op jit(solution)/shard_map/all_to_all | solution.py:74
  155.7 8.8 %all-to-all-start.1 = ((f32[8,128,1]{1,2,0:T(1,128)}), f32[8,128,1]{1,2,0:T(1,128)S(1)}, u32[]{:S(2)}, u32[]{:S(2)}) async-start(f32[8,128,1]{1,2,0:T(1,128)} %all_to_all.20), calls=%async_computation.1 | async-start | bytes 8192 | tf_op jit(solution)/shard_map/all_to_all | solution.py:75
  159.6 25.7 %collective-permute-start.1 = (f32[1]{0:T(128)S(1)}, f32[1]{0:T(128)}, u32[]{:S(2)}, u32[]{:S(2)}) collective-permute-start(f32[1]{0:T(128)S(1)} %bitcast.85), channel_id=1, source_target_pairs={{4,0},{8,4},{12,8},{16,12},{20,16},{24,20},{28,24},{5,1},{9,5},{13... | collective-permute-start | bytes 20 | tf_op jit(solution)/shard_map/ppermute | solution.py:26
  164.5 9.8 %all-to-all-start.2 = ((f32[8,128,1]{1,2,0:T(1,128)}), f32[8,128,1]{1,2,0:T(1,128)S(1)}, u32[]{:S(2)}, u32[]{:S(2)}) async-start(f32[8,128,1]{1,2,0:T(1,128)} %all_to_all.22), calls=%async_computation.2 | async-start | bytes 8192 | tf_op jit(solution)/shard_map/all_to_all | solution.py:76
  608.3 10.8 %collective-permute-start = (f32[1]{0:T(128)}, f32[1]{0:T(128)}, u32[]{:S(2)}, u32[]{:S(2)}) collective-permute-start(f32[1]{0:T(128)} %add.147), channel_id=1, source_target_pairs={{4,0},{8,4},{12,8},{16,12},{20,16},{24,20},{28,24},{5,1},{9,5},{13... | collective-permute-start | bytes 20 | tf_op jit(solution)/shard_map/while/body/eval_jaxpr/ppermute | solution.py:26
  619.8 4.8 collective-permute-start
  625.2 4.8 collective-permute-start
  630.7 4.8 collective-permute-start
  636.2 4.8 collective-permute-start
  641.7 4.8 collective-permute-start
  647.2 4.8 collective-permute-start
Sparse Core Ops, SparseCore 0:
  12.3 84.4 all-gather.7
where the time goes:
time: 664 us; the launch traced here: 660 us
  loops' own time  242 us (36%)
  local copies, waits for them, and re-layouts  187 us (28%)
  waiting for transfers between devices  104 us (16%)
  matrix products  48.5 us (7%)
  starting transfers between devices  39.4 us (6%)
  blocking collectives  16.7 us (3%)
  between operations  14.1 us (2%)
  other arithmetic  7.76 us (1%)
    another operation x1, loops' own time, per_device(): lax.scan(backward, (jnp.zeros((), jnp.float32), jnp.ones((), jnp.float32)...  237 us
    dynamic_slice x256, local copies, waits for them, and re-layouts, per_device(): lax.scan(backward, (jnp.zeros((), jnp.float32), jnp.ones((), jnp.float32)...  155 us
    all_gather x1, waiting for transfers between devices, per_device(): gathered = lax.all_gather(normed, 'batch', axis=0, tiled=True)  83.9 us
    dot_general x2, matrix products, score_block(): logits = jnp.dot(rows_block, unembed, preferred_element_type=jnp.float32)  45.2 us
    dynamic_update_slice x256, local copies, waits for them, and re-layouts, per_device(): lax.scan(backward, (jnp.zeros((), jnp.float32), jnp.ones((), jnp.float32)...  29.4 us
    ppermute x8, starting transfers between devices, from_behind(): lax.ppermute(value, axis, [(source, source + steps) for source in range(i...  28.2 us
    all_gather x3, blocking collectives, joined(): gathered = jax.tree.map(lambda a: lax.all_gather(a, axis), part)  16.7 us
    ppermute x8, waiting for transfers between devices, from_behind(): lax.ppermute(value, axis, [(source, source + steps) for source in range(i...  13.7 us
  transfers between devices with their start and end apart: 12, of which 10 were waited for; matrix products, arithmetic and copies ran while one was open for 0% of the time, Pallas kernels for 0%

commit v1 on v0

--- a/solution.py
+++ b/solution.py
@@ -47,7 +47,13 @@
     peers = lax.axis_size("batch")
     width = hidden.shape[1]
     normed = normalize(hidden, exit_layer, exit_gains)
-    gathered = lax.all_gather(normed, "batch", axis=0, tiled=True)
+    x = normed
+    ways, here, step = (lax.axis_size("batch"), lax.axis_index("batch"), x.shape[0])
+    lengths = [n * ways if d == 0 else n for d, n in enumerate(x.shape)]
+    gathered = lax.dynamic_update_slice_in_dim(jnp.zeros(lengths, x.dtype), x, here * step, axis=0)
+    for far in range(1, ways):
+        x = lax.ppermute(x, "batch", [(d, (d + 1) % ways) for d in range(ways)])
+        gathered = lax.dynamic_update_slice_in_dim(gathered, x, (here - far) % ways * step, axis=0)
     block_rows = 512
     block_count = total_rows // block_rows
 

time: 664 us -> 683 us (1.029)
  starting transfers between devices: 39.4 us -> 69.2 us
  between operations: 14.1 us -> 0.81 us
  local copies, waits for them, and re-layouts: 187 us -> 199 us
  waiting for transfers between devices: 104 us -> 95.8 us
    all_gather x1 -> x0, waiting for transfers between devices: 83.9 us -> none  [per_device(): gathered = lax.all_gather(normed, 'batch', axis=0, tiled=True)]
    ppermute x0 -> x7, waiting for transfers between devices: none -> 73.6 us  [per_device(): x = lax.ppermute(x, 'batch', [(d, (d + 1) % ways) for d in range(ways)])]
    ppermute x0 -> x7, starting transfers between devices: none -> 17.5 us  [per_device(): x = lax.ppermute(x, 'batch', [(d, (d + 1) % ways) for d in range(ways)])]
    all_to_all x1, starting transfers between devices: 3.43 us -> 16.6 us  [per_device(): lax.all_to_all(maxima, 'batch', split_axis=0, concat_axis=0, tiled=True)]
    dynamic_update_slice x0 -> x7, local copies, waits for them, and re-layouts: none -> 9.88 us  [per_device(): lax.dynamic_update_slice_in_dim(gathered, x, (here - far) % ways * step,...]
  transfers between devices with their start and end apart: 12 -> 18, of which waited for: 10 -> 16; matrix products, arithmetic and copies ran while one was open for 0% -> 1% of each run, Pallas kernels for 0% -> 0%
where the time goes in v1:
time: 683 us; the launch traced here: 679 us
  loops' own time  242 us (35%)
  local copies, waits for them, and re-layouts  199 us (29%)
  waiting for transfers between devices  95.8 us (14%)
  starting transfers between devices  69.2 us (10%)
  matrix products  47.3 us (7%)
  blocking collectives  17.2 us (3%)
  other arithmetic  7.88 us (1%)
    another operation x1, loops' own time, per_device(): lax.scan(backward, (jnp.zeros((), jnp.float32), jnp.ones((), jnp.float32)...  237 us
    dynamic_slice x256, local copies, waits for them, and re-layouts, per_device(): lax.scan(backward, (jnp.zeros((), jnp.float32), jnp.ones((), jnp.float32)...  153 us
    ppermute x7, waiting for transfers between devices, per_device(): x = lax.ppermute(x, 'batch', [(d, (d + 1) % ways) for d in range(ways)])  73.6 us
    dot_general x2, matrix products, score_block(): logits = jnp.dot(rows_block, unembed, preferred_element_type=jnp.float32)  45.2 us
    dynamic_update_slice x256, local copies, waits for them, and re-layouts, per_device(): lax.scan(backward, (jnp.zeros((), jnp.float32), jnp.ones((), jnp.float32)...  29.4 us
    ppermute x8, starting transfers between devices, from_behind(): lax.ppermute(value, axis, [(source, source + steps) for source in range(i...  27.3 us
    ppermute x7, starting transfers between devices, per_device(): x = lax.ppermute(x, 'batch', [(d, (d + 1) % ways) for d in range(ways)])  17.5 us
    all_gather x3, blocking collectives, joined(): gathered = jax.tree.map(lambda a: lax.all_gather(a, axis), part)  17.2 us
  transfers between devices with their start and end apart: 18, of which 16 were waited for; matrix products, arithmetic and copies ran while one was open for 1% of the time, Pallas kernels for 0%

profile of v1, /device:TPU:1, one launch (start us, length us, event | category | flops | bytes accessed | tf_op | source)
XLA Modules:
  0.0 679.3 jit_solution(4155783967231851121)
XLA Ops:
  2.3 4.3 broadcast_in_dim.43
  6.6 2.1 constant_dynamic-update-slice_fusion.7
  8.7 2.6 collective-permute-start.1
  11.3 11.7 %collective-permute-done.1 = bf16[128,4096]{1,0:T(8,128)(2,1)S(1)} collective-permute-done((bf16[128,4096]{1,0:T(8,128)(2,1)S(1)}, bf16[128,4096]{1,0:T(8,128)(2,1)S(1)}, u32[]{:S(2)}, u32[]{:S(2)}) %collective-permute-start.1) | collective-permute-done | bytes 1048608 | tf_op jit(solution)/shard_map/ppermute | solution.py:55
  23.1 2.5 collective-permute-start.2
  25.6 11.7 %collective-permute-done.2 = bf16[128,4096]{1,0:T(8,128)(2,1)S(1)} collective-permute-done((bf16[128,4096]{1,0:T(8,128)(2,1)S(1)}, bf16[128,4096]{1,0:T(8,128)(2,1)S(1)}, u32[]{:S(2)}, u32[]{:S(2)}) %collective-permute-start.2) | collective-permute-done | bytes 1048608 | tf_op jit(solution)/shard_map/ppermute | solution.py:55
  37.3 2.5 collective-permute-start.3
  39.8 11.7 %collective-permute-done.3 = bf16[128,4096]{1,0:T(8,128)(2,1)S(1)} collective-permute-done((bf16[128,4096]{1,0:T(8,128)(2,1)S(1)}, bf16[128,4096]{1,0:T(8,128)(2,1)S(1)}, u32[]{:S(2)}, u32[]{:S(2)}) %collective-permute-start.3) | collective-permute-done | bytes 1048608 | tf_op jit(solution)/shard_map/ppermute | solution.py:55
  51.5 2.5 collective-permute-start.4
  54.0 11.7 %collective-permute-done.4 = bf16[128,4096]{1,0:T(8,128)(2,1)S(1)} collective-permute-done((bf16[128,4096]{1,0:T(8,128)(2,1)S(1)}, bf16[128,4096]{1,0:T(8,128)(2,1)S(1)}, u32[]{:S(2)}, u32[]{:S(2)}) %collective-permute-start.4) | collective-permute-done | bytes 1048608 | tf_op jit(solution)/shard_map/ppermute | solution.py:55
  65.8 2.5 collective-permute-start.5
  68.3 11.7 %collective-permute-done.5 = bf16[128,4096]{1,0:T(8,128)(2,1)} collective-permute-done((bf16[128,4096]{1,0:T(8,128)(2,1)S(1)}, bf16[128,4096]{1,0:T(8,128)(2,1)}, u32[]{:S(2)}, u32[]{:S(2)}) %collective-permute-start.5) | collective-permute-done | bytes 1048608 | tf_op jit(solution)/shard_map/ppermute | solution.py:55
  80.0 2.6 collective-permute-start.6
  84.7 2.3 constant_dynamic-update-slice_fusion.4
  87.0 7.6 %collective-permute-done.6 = bf16[128,4096]{1,0:T(8,128)(2,1)S(1)} collective-permute-done((bf16[128,4096]{1,0:T(8,128)(2,1)}, bf16[128,4096]{1,0:T(8,128)(2,1)S(1)}, u32[]{:S(2)}, u32[]{:S(2)}) %collective-permute-start.6) | collective-permute-done | bytes 1048608 | tf_op jit(solution)/shard_map/ppermute | solution.py:55
  94.6 2.4 collective-permute-start.7
  98.1 2.3 constant_dynamic-update-slice_fusion.2
  101.4 7.3 %collective-permute-done.7 = bf16[128,4096]{1,0:T(8,128)(2,1)S(1)} collective-permute-done((bf16[128,4096]{1,0:T(8,128)(2,1)S(1)}, bf16[128,4096]{1,0:T(8,128)(2,1)S(1)}, u32[]{:S(2)}, u32[]{:S(2)}) %collective-permute-start.7) | collective-permute-done | bytes 1048608 | tf_op jit(solution)/shard_map/ppermute | solution.py:55
  109.8 49.9 %while.67 = (s32[]{:T(128)}, f32[2,512]{1,0:T(2,128)S(1)}, f32[2,512]{1,0:T(2,128)S(1)}, f32[2,512]{1,0:T(2,128)S(1)}, bf16[2,512,4096]{2,1,0:T(8,128)(2,1)}, /*...) while((s32[]{:T(128)}, f32[2,512]{1,0:T(2,128)S(1)}, ...), condition=%wide.region_5.6_spmd.clone, body=%wide.region_1.5_spmd.clone.sunk | while | flops 16823081984 | bytes 53471864 | solution.py:69
  109.8 22.6 %fusion.28 = (f32[512]{0:T(512)S(1)}, f32[512,4008]{0,1:T(8,128)S(1)}) fusion(bf16[4096,4008]{0,1:T(8,128)(2,1)} %get-tuple-element.683, bf16[2,512,4096]{2,1,0:T(8,128)(2,1)} %get-tuple-element.682, s32[]{:T(128)} %get-tuple-element.668), kind=kOutput, calls=%fused_computation.46.clone.1 | convolution fusion | flops 16812822528 | bytes 45238784 | tf_op jit(solution)/shard_map/while/body/eval_jaxpr/dot_general | solution.py:62
  132.4 2.2 select_reduce_fusion.2
  134.8 22.6 %fusion.28 = (f32[512]{0:T(512)S(1)}, f32[512,4008]{0,1:T(8,128)S(1)}) fusion(bf16[4096,4008]{0,1:T(8,128)(2,1)} %get-tuple-element.683, bf16[2,512,4096]{2,1,0:T(8,128)(2,1)} %get-tuple-element.682, s32[]{:T(128)} %get-tuple-element.668), kind=kOutput, calls=%fused_computation.46.clone.1 | convolution fusion | flops 16812822528 | bytes 45238784 | tf_op jit(solution)/shard_map/while/body/eval_jaxpr/dot_general | solution.py:62
  157.4 2.2 select_reduce_fusion.2
  160.3 16.6 %all-to-all-start = ((f32[8,128,1]{1,2,0:T(1,128)}), f32[8,128,1]{1,2,0:T(1,128)S(1)}, u32[]{:S(2)}, u32[]{:S(2)}) async-start(f32[8,128,1]{1,2,0:T(1,128)} %all_to_all.18), calls=%async_computation | async-start | bytes 8192 | tf_op jit(solution)/shard_map/all_to_all | solution.py:80
  177.5 4.3 all-to-all-done
  181.8 3.9 all-to-all-start.1
  185.7 2.0 collective-permute-start.8
  188.4 2.2 all-to-all-done.1
  190.6 3.9 all-to-all-start.2
  194.5 6.4 all-gather.4
  200.9 5.9 all-gather.5
  206.8 4.9 all-gather.3
  213.1 419.8 %while.65 = (s32[]{:T(128)}, f32[]{:T(128)}, f32[]{:T(128)}, f32[128]{0:T(128)S(1)}, f32[128]{0:T(128)S(1)}, /*index=5*/f32[128]{0:T(128)S(1)}, f32[128]{0:T(128)S(1)}, s32[]{:T(128)}, s32[]{:T(128)}) while((s32[]{:T(128)}, f32[]{:T(128)}, f32[]{:T(128)}, f32[128]{0:T(128)S(1)}, f32[128]{0:T(128)S(1)}, /*index=5*/f32[128]{0:T(128)S(1)}, ...), condition=%wide.region_12.13_spmd, body=%wide.region_11.12_spmd.sunk | while | flops 6 | bytes 189 | solution.py:113
  632.9 45.9 %while.66 = (s32[]{:T(128)}, f32[1]{0:T(128)}, f32[1]{0:T(128)S(1)}, f32[1]{0:T(128)S(1)}, s32[]{:T(128)}) while((s32[]{:T(128)}, f32[1]{0:T(128)}, f32[1]{0:T(128)S(1)}, f32[1]{0:T(128)S(1)}, s32[]{:T(128)}) %tuple.127), condition=%wide.region_14.15_spmd, body=%wide.region_13.14_spmd.sunk | while | flops 4 | bytes 141 | solution.py:126
  633.0 8.9 %collective-permute-start = (f32[1]{0:T(128)}, f32[1]{0:T(128)}, u32[]{:S(2)}, u32[]{:S(2)}) collective-permute-start(f32[1]{0:T(128)} %add.215), channel_id=1, source_target_pairs={{4,0},{8,4},{12,8},{16,12},{20,16},{24,20},{28,24},{5,1},{9,5},{13... | collective-permute-start | bytes 20 | tf_op jit(solution)/shard_map/while/body/eval_jaxpr/ppermute | solution.py:26
  641.9 2.1 collective-permute-done
  644.7 2.7 collective-permute-start
  647.4 2.3 collective-permute-done
  650.4 2.7 collective-permute-start
  653.1 2.3 collective-permute-done
  656.1 2.7 collective-permute-start
  658.8 2.3 collective-permute-done
  661.8 2.7 collective-permute-start
  664.5 2.3 collective-permute-done
  667.5 2.7 collective-permute-start
  670.2 2.3 collective-permute-done
  673.2 2.7 collective-permute-start
  675.9 2.3 collective-permute-done
  (569 shorter events, 193.8 us)
Async XLA Ops:
  0.6 5.9 copy-start
  0.6 5.9 copy-start.1
  0.7 5.9 copy-start.4
  0.7 67.6 %copy-start.3 = (s32[1024]{0:T(1024)S(1)}, s32[1024]{0:T(1024)}, u32[]{:S(2)}) copy-start(s32[1024]{0:T(1024)} %param.21) | copy-start | bytes 12292
  8.7 14.4 %collective-permute-start.1 = (bf16[128,4096]{1,0:T(8,128)(2,1)S(1)}, bf16[128,4096]{1,0:T(8,128)(2,1)S(1)}, u32[]{:S(2)}, u32[]{:S(2)}) collective-permute-start(bf16[128,4096]{1,0:T(8,128)(2,1)S(1)} %get-tuple-element.483), channel_id=1, source_target_pairs={{0,4},{4,8},{8,12},{12,16},{16,20},{20,24},{24,28},{28,0},{1,5},{5... | collective-permute-start | bytes 3145736 | tf_op jit(solution)/shard_map/ppermute | solution.py:55
  23.1 14.2 %collective-permute-start.2 = (bf16[128,4096]{1,0:T(8,128)(2,1)S(1)}, bf16[128,4096]{1,0:T(8,128)(2,1)S(1)}, u32[]{:S(2)}, u32[]{:S(2)}) collective-permute-start(bf16[128,4096]{1,0:T(8,128)(2,1)S(1)} %collective-permute-done.1), channel_id=1, source_target_pairs={{0,4},{4,8},{8,12},{12,16},{16,20},{20,24},{24,28},{28,0},{1,5},{5... | collective-permute-start | bytes 3145736 | tf_op jit(solution)/shard_map/ppermute | solution.py:55
  37.3 14.2 %collective-permute-start.3 = (bf16[128,4096]{1,0:T(8,128)(2,1)S(1)}, bf16[128,4096]{1,0:T(8,128)(2,1)S(1)}, u32[]{:S(2)}, u32[]{:S(2)}) collective-permute-start(bf16[128,4096]{1,0:T(8,128)(2,1)S(1)} %collective-permute-done.2), channel_id=1, source_target_pairs={{0,4},{4,8},{8,12},{12,16},{16,20},{20,24},{24,28},{28,0},{1,5},{5... | collective-permute-start | bytes 3145736 | tf_op jit(solution)/shard_map/ppermute | solution.py:55
  51.5 14.2 %copy-start.2 = (bf16[128,4096]{1,0:T(8,128)(2,1)}, bf16[128,4096]{1,0:T(8,128)(2,1)S(1)}, u32[]{:S(2)}) copy-start(bf16[128,4096]{1,0:T(8,128)(2,1)S(1)} %collective-permute-done.3) | copy-start | bytes 3145732
  51.5 14.2 %collective-permute-start.4 = (bf16[128,4096]{1,0:T(8,128)(2,1)S(1)}, bf16[128,4096]{1,0:T(8,128)(2,1)S(1)}, u32[]{:S(2)}, u32[]{:S(2)}) collective-permute-start(bf16[128,4096]{1,0:T(8,128)(2,1)S(1)} %collective-permute-done.3), channel_id=1, source_target_pairs={{0,4},{4,8},{8,12},{12,16},{16,20},{20,24},{24,28},{28,0},{1,5},{5... | collective-permute-start | bytes 3145736 | tf_op jit(solution)/shard_map/ppermute | solution.py:55
  65.8 14.2 %collective-permute-start.5 = (bf16[128,4096]{1,0:T(8,128)(2,1)S(1)}, bf16[128,4096]{1,0:T(8,128)(2,1)}, u32[]{:S(2)}, u32[]{:S(2)}) collective-permute-start(bf16[128,4096]{1,0:T(8,128)(2,1)S(1)} %collective-permute-done.4), channel_id=1, source_target_pairs={{0,4},{4,8},{8,12},{12,16},{16,20},{20,24},{24,28},{28,0},{1,5},{5... | collective-permute-start | bytes 3145736 | tf_op jit(solution)/shard_map/ppermute | solution.py:55
  80.0 14.6 %collective-permute-start.6 = (bf16[128,4096]{1,0:T(8,128)(2,1)}, bf16[128,4096]{1,0:T(8,128)(2,1)S(1)}, u32[]{:S(2)}, u32[]{:S(2)}) collective-permute-start(bf16[128,4096]{1,0:T(8,128)(2,1)} %collective-permute-done.5), channel_id=1, source_target_pairs={{0,4},{4,8},{8,12},{12,16},{16,20},{20,24},{24,28},{28,0},{1,5},{5... | collective-permute-start | bytes 3145736 | tf_op jit(solution)/shard_map/ppermute | solution.py:55
  94.6 14.1 %collective-permute-start.7 = (bf16[128,4096]{1,0:T(8,128)(2,1)S(1)}, bf16[128,4096]{1,0:T(8,128)(2,1)S(1)}, u32[]{:S(2)}, u32[]{:S(2)}) collective-permute-start(bf16[128,4096]{1,0:T(8,128)(2,1)S(1)} %collective-permute-done.6), channel_id=1, source_target_pairs={{0,4},{4,8},{8,12},{12,16},{16,20},{20,24},{24,28},{28,0},{1,5},{5... | collective-permute-start | bytes 3145736 | tf_op jit(solution)/shard_map/ppermute | solution.py:55
  109.8 75.9 %copy-start.5 = (f32[128]{0:T(128)S(1)}, f32[128]{0:T(128)}, u32[]{:S(2)}) copy-start(f32[128]{0:T(128)} %param.22) | copy-start | bytes 1540
  109.8 102.1 %copy-start.6 = (f32[128]{0:T(128)S(1)}, f32[128]{0:T(128)}, u32[]{:S(2)}) copy-start(f32[128]{0:T(128)} %param.23) | copy-start | bytes 1540
  109.8 102.1 %copy-start.7 = (f32[128]{0:T(128)S(1)}, f32[128]{0:T(128)}, u32[]{:S(2)}) copy-start(f32[128]{0:T(128)} %param.24) | copy-start | bytes 1540
  109.8 102.1 %copy-start.8 = (s32[128]{0:T(128)S(1)}, s32[128]{0:T(128)}, u32[]{:S(2)}) copy-start(s32[128]{0:T(128)} %param.25) | copy-start | bytes 1540
  160.3 21.5 %all-to-all-start = ((f32[8,128,1]{1,2,0:T(1,128)}), f32[8,128,1]{1,2,0:T(1,128)S(1)}, u32[]{:S(2)}, u32[]{:S(2)}) async-start(f32[8,128,1]{1,2,0:T(1,128)} %all_to_all.18), calls=%async_computation | async-start | bytes 8192 | tf_op jit(solution)/shard_map/all_to_all | solution.py:80
  181.8 8.8 %all-to-all-start.1 = ((f32[8,128,1]{1,2,0:T(1,128)}), f32[8,128,1]{1,2,0:T(1,128)S(1)}, u32[]{:S(2)}, u32[]{:S(2)}) async-start(f32[8,128,1]{1,2,0:T(1,128)} %all_to_all.20), calls=%async_computation.1 | async-start | bytes 8192 | tf_op jit(solution)/shard_map/all_to_all | solution.py:81
  185.7 26.2 %collective-permute-start.8 = (f32[1]{0:T(128)S(1)}, f32[1]{0:T(128)}, u32[]{:S(2)}, u32[]{:S(2)}) collective-permute-start(f32[1]{0:T(128)S(1)} %bitcast.85), channel_id=1, source_target_pairs={{4,0},{8,4},{12,8},{16,12},{20,16},{24,20},{28,24},{5,1},{9,5},{13... | collective-permute-start | bytes 20 | tf_op jit(solution)/shard_map/ppermute | solution.py:26
  190.6 10.3 %all-to-all-start.2 = ((f32[8,128,1]{1,2,0:T(1,128)}), f32[8,128,1]{1,2,0:T(1,128)S(1)}, u32[]{:S(2)}, u32[]{:S(2)}) async-start(f32[8,128,1]{1,2,0:T(1,128)} %all_to_all.22), calls=%async_computation.2 | async-start | bytes 8192 | tf_op jit(solution)/shard_map/all_to_all | solution.py:82
  633.0 11.0 %collective-permute-start = (f32[1]{0:T(128)}, f32[1]{0:T(128)}, u32[]{:S(2)}, u32[]{:S(2)}) collective-permute-start(f32[1]{0:T(128)} %add.215), channel_id=1, source_target_pairs={{4,0},{8,4},{12,8},{16,12},{20,16},{24,20},{28,24},{5,1},{9,5},{13... | collective-permute-start | bytes 20 | tf_op jit(solution)/shard_map/while/body/eval_jaxpr/ppermute | solution.py:26
  644.7 5.0 collective-permute-start
  650.4 5.0 collective-permute-start
  656.1 5.0 collective-permute-start
  661.8 5.0 collective-permute-start
  667.5 5.0 collective-permute-start
  673.2 5.0 collective-permute-start
